TPU v7x, 32 devices: a whole 2x2x4 slice. The times are simulated.
32 devices in a mesh: groups: 2 (over x), blk: 16 (over z, y, core).
Axes of the slice: x: 2, y: 2, z: 4, core: 2. Of those that a mesh axis runs over, the one named last changes fastest.
Arguments:
- queries: float32 [64, 8192], P(('groups', 'blk')), parts along dimension 0, may hold values from -50 to 50
- prefix_keys: float32 [4096, 512], P(('groups', 'blk')), parts along dimension 0, may hold values from -40 to 40
- prefix_values: float32 [4096, 512], P(('groups', 'blk')), parts along dimension 0, may hold values from -8 to 8
- out_weight: float32 [8192, 4096], P('blk'), may hold values from -0.0625 to 0.0625
- lengths: int32 [4], P('groups'), parts along dimension 0, may hold values from 512 to 2048, as said below
Outputs:
- mixed: float32 [64, 4096], P(('groups', 'blk')), parts along dimension 0
There are 2 independent parts, one for each index of `groups`. A program takes and returns all parts, laid end to end along the dimension named above; an argument that names none is the same for every part. Nothing has to cross between parts.
Inputs may be any that keep to these rules, and one draw needn't show every extreme that they name: `lengths`: each request sees at least the first 512 prefix tokens, and some request sees all 2048 of them.
All inputs are finite; a program needn't handle non-finite values.
Results may differ from a plain program's by a relative error of at most 0.0003.
Values sent between devices are 32-bit elements; how exact they have to be, the bound alone decides.
No kernel may reach another device: no remote copies, remote signals or barrier semaphores. Data moves between devices by JAX's collectives and lax.ppermute only.
A program may use at most 128 MiB of HBM per device.

v0:
```python
import functools
import math

import jax
import jax.numpy as jnp
from jax import lax
from jax.experimental import pallas as pl
from jax.experimental.pallas import tpu as pltpu
from jax.sharding import PartitionSpec as P


H = 64
KVH = 4
HD = 128
REQ_TOK = 16
GROUP = H // KVH
PLANE_BITS = KVH.bit_length() - 1
LANES = 128

HIGHEST = lax.Precision.HIGHEST
NEG_FILL = -1e30


VMEM = pltpu.VMEM


def relative(order, bits):
    out = 0
    for b in range(PLANE_BITS):
        out = out + (((order >> (PLANE_BITS - 1 - b)) & 1) << (bits + b))
    for b in range(bits):
        out = out + (((order >> (PLANE_BITS + bits - 1 - b)) & 1) << b)
    return out


def swap_rows(x, size):
    blocks = [x[i * size : (i + 1) * size] for i in range(x.shape[0] // size)]
    return jnp.concatenate([blocks[i ^ 1] for i in range(len(blocks))], axis=0)


def stats_tile(columns, rows):
    lane = lax.broadcasted_iota(jnp.int32, (8, LANES), 1)
    out = jnp.zeros((8, LANES), jnp.float32)
    for g in range(rows // 8):
        for i, column in enumerate(columns):
            out = jnp.where(lane == g * len(columns) + i, column[8 * g : 8 * g + 8], out)
    return out


def stats_column(tile, i, count, rows):
    return jnp.concatenate([tile[:, g * count + i :][:, :1] for g in range(rows // 8)], axis=0)


def pieces_of(x, count):
    out = []
    for _ in range(count):
        out.append(x.astype(jnp.bfloat16))
        x = x - out[-1].astype(jnp.float32)
    return out


def times(a, b, dims=(((1,), (0,)), ((), ()))):
    return lax.dot_general(a, b, dims, preferred_element_type=jnp.float32)


def limit(mib):
    return pltpu.CompilerParams(vmem_limit_bytes=mib << 20)


IN_VMEM = pl.BlockSpec(memory_space=VMEM)
IN_PLACE = pl.BlockSpec(memory_space=pl.ANY)


def in_hbm(x):
    return pltpu.with_memory_space_constraint(x, pltpu.HBM)


def run_copies(pairs, sems):
    copies = [pltpu.make_async_copy(src, dst, sems.at[i]) for i, (src, dst) in enumerate(pairs)]
    for copy in copies:
        copy.start()
    return copies


def pack_q_kernel(bits, len_hbm, q_hbm, *refs):
    q_outs, (limit_out, len_ref, sems) = refs[:-3], refs[-3:]
    position = lax.axis_index("blk")
    wide, half = GROUP * HD, KVH // 2
    pairs = [(len_hbm, len_ref)]
    for step in reversed(range(KVH)):
        lanes = pl.ds(pl.multiple_of(((position >> bits) ^ step) * wide, wide), wide)
        q_out = q_outs[0].at[:, pl.ds((step - half) * wide, wide)] if step >= half else q_outs[1 + step]
        pairs.append((q_hbm.at[:, lanes], q_out))
    copies = run_copies(pairs, sems)
    local_rows = q_hbm.shape[0]
    row = lax.broadcasted_iota(jnp.int32, limit_out.shape, 0)
    token = (position ^ relative(row // local_rows, bits)) * local_rows + row % local_rows
    request = token // REQ_TOK
    copies[0].wait()
    limits = jnp.zeros(limit_out.shape, jnp.int32)
    for i in range(len_ref.shape[0]):
        limits = jnp.where(request == i, len_ref[i], limits)
    limit_out[...] = limits
    for copy in copies[1:]:
        copy.wait()


def pack_q(bits, lengths, queries):
    local_rows, wide = queries.shape[0], GROUP * HD
    q_high = jax.ShapeDtypeStruct((local_rows, KVH // 2 * wide), jnp.float32)
    q = jax.ShapeDtypeStruct((local_rows, wide), jnp.float32)
    limits = jax.ShapeDtypeStruct(((KVH << bits) * local_rows, LANES), jnp.int32)
    out = pl.pallas_call(
        functools.partial(pack_q_kernel, bits),
        out_shape=[q_high] + [q] * (KVH // 2) + [limits],
        in_specs=[IN_PLACE] * 2,
        out_specs=[IN_VMEM] * (KVH // 2 + 2),
        scratch_shapes=[pltpu.SMEM(lengths.shape, jnp.int32), pltpu.SemaphoreType.DMA((1 + KVH,))],
        compiler_params=limit(4),
        name="pack_q",
    )(in_hbm(lengths), in_hbm(queries))
    return out[:-1], out[-1]


def pack_kv_kernel(bits, k_hbm, v_hbm, *refs):
    kv_outs, sems = refs[:-1], refs[-1]
    plane = lax.axis_index("blk") >> bits
    keys = k_hbm.shape[0]
    pairs = []
    for step in reversed(range(KVH)):
        lanes = pl.ds(pl.multiple_of((plane ^ step) * HD, HD), HD)
        pairs.append((k_hbm.at[:, lanes], kv_outs[step].at[pl.ds(0, keys), :]))
        pairs.append((v_hbm.at[:, lanes], kv_outs[step].at[pl.ds(keys, keys), :]))
    for copy in run_copies(pairs, sems):
        copy.wait()


def pack_kv(bits, keys, values):
    kv = jax.ShapeDtypeStruct((2 * keys.shape[0], HD), jnp.float32)
    return pl.pallas_call(
        functools.partial(pack_kv_kernel, bits),
        out_shape=[kv] * KVH,
        in_specs=[IN_PLACE] * 2,
        out_specs=[IN_VMEM] * KVH,
        scratch_shapes=[pltpu.SemaphoreType.DMA((2 * KVH,))],
        compiler_params=limit(4),
        cost_estimate=pl.CostEstimate(flops=0, bytes_accessed=16 * keys.size, transcendentals=0),
        name="pack_kv",
    )(in_hbm(keys), in_hbm(values))


def split_kernel(first, tile, w_hbm, high_ref, low_ref, buf, sems):
    chunks = buf.shape[0]
    copies = [
        pltpu.make_async_copy(w_hbm.at[pl.ds(first + c * tile, tile), :], buf.at[c], sems.at[c])
        for c in range(chunks)
    ]
    for copy in copies:
        copy.start()
    for c in range(chunks):
        copies[c].wait()
        rows = slice(c * tile, (c + 1) * tile)
        high_ref[rows, :], low_ref[rows, :] = pieces_of(buf[c], 2)


def split_weight(weight, first, count):
    width = weight.shape[1]
    tile = min(count, 64)
    out = jax.ShapeDtypeStruct((count, width), jnp.bfloat16)
    return pl.pallas_call(
        functools.partial(split_kernel, first, tile),
        out_shape=[out, out],
        in_specs=[IN_PLACE],
        out_specs=[IN_VMEM] * 2,
        scratch_shapes=[
            pltpu.VMEM((count // tile, tile, width), jnp.float32),
            pltpu.SemaphoreType.DMA((count // tile,)),
        ],
        compiler_params=limit(12),
        cost_estimate=pl.CostEstimate(
            flops=8 * count * width, bytes_accessed=8 * count * width, transcendentals=0
        ),
        name="split",
    )(in_hbm(weight))


def attend_kernel(bits, key_count, rels, limit_ref, *refs):
    sub = 1 << bits
    inputs, outs = refs[: -len(rels)], refs[-len(rels) :]
    q_refs, kv_refs = inputs[:-KVH], inputs[-KVH:]
    position = lax.axis_index("blk")
    plane, place = position // sub, position % sub
    rows = limit_ref.shape[0]
    per_owner = GROUP // sub
    held = key_count * KVH

    at = lax.broadcasted_iota(jnp.int32, (1, held), 1)
    source = (plane ^ (at // key_count)) * sub + place
    visible = (source * key_count + at % key_count) < limit_ref[:, :1]

    keys = jnp.concatenate([r[:key_count, :] for r in kv_refs], axis=0)
    values = jnp.concatenate([r[key_count:, :] for r in kv_refs], axis=0)
    k1, k2, k3 = pieces_of(keys, 3)
    k12, k31 = jnp.concatenate([k1, k2], axis=1), jnp.concatenate([k3, k1], axis=1)
    v1, v2 = pieces_of(values, 2)
    v12 = jnp.concatenate([v1, v2], axis=1)
    both = (((1,), (1,)), ((), ()))
    scale = 1.0 / math.sqrt(HD)

    count = len(rels) * per_owner
    cross = jnp.broadcast_to(visible[None], (count, rows, held))
    heads = []
    for rel in rels:
        for i in range(per_owner):
            lanes = pl.ds(pl.multiple_of(((place ^ rel) * per_owner + i) * HD, HD), HD)
            heads += [q_ref[:, lanes] for q_ref in q_refs]
    q1, q2, q3 = pieces_of(jnp.concatenate(heads, axis=0), 3)
    q11, q22 = jnp.concatenate([q1, q1], axis=1), jnp.concatenate([q2, q2], axis=1)
    q13 = jnp.concatenate([q1, q3], axis=1)
    scores = times(q11, k12, both) + (times(q22, k12, both) + times(q13, k31, both))
    scores = scores.reshape(count, rows, held) * scale
    masked = jnp.where(cross, scores, NEG_FILL)
    peak = jnp.max(masked, axis=2, keepdims=True)
    weights = jnp.where(cross, jnp.exp(masked - peak), 0.0)
    total = jnp.sum(weights, axis=2, keepdims=True)
    w1, w2 = pieces_of(weights.reshape(count * rows, held), 2)
    wide = times(w1, v12)
    sums = wide[:, :HD] + (wide[:, HD:] + times(w2, v1))
    for n, ref in enumerate(outs):
        own = range(n * per_owner, (n + 1) * per_owner)
        ref[: per_owner * rows, :] = sums[own.start * rows : own.stop * rows]
        ref[per_owner * rows :, :] = stats_tile([peak[h] for h in own] + [total[h] for h in own], rows)


def attend(bits, rels, limits, q_parts, kv_held):
    rows, key_count = limits.shape[0], kv_held[0].shape[0] // 2
    height = rows * (GROUP >> bits)
    pairs = rows * (GROUP >> bits) * len(rels) * key_count * KVH
    return pl.pallas_call(
        functools.partial(attend_kernel, bits, key_count, rels),
        out_shape=[jax.ShapeDtypeStruct((height + 8, HD), jnp.float32)] * len(rels),
        in_specs=[IN_VMEM] * (1 + len(q_parts) + KVH),
        out_specs=[IN_VMEM] * len(rels),
        compiler_params=limit(16),
        cost_estimate=pl.CostEstimate(
            flops=12 * pairs * HD, bytes_accessed=4 * height * HD, transcendentals=pairs
        ),
        name="attend",
    )(limits, *q_parts, *kv_held)


def merged(parts, heads):
    rows = (parts[0][0].shape[0] - 8) // heads

    def ordered(x, sizes):
        return functools.reduce(swap_rows, sizes, x)

    tiles = [(ref[heads * rows :, :], sizes) for ref, sizes in parts]

    def stat(i):
        return [ordered(stats_column(tile, i, 2 * heads, rows), sizes) for tile, sizes in tiles]

    sums, totals = [], []
    for i in range(heads):
        peaks = stat(i)
        peak = functools.reduce(jnp.maximum, peaks)
        factors = [jnp.exp(x - peak) for x in peaks]
        held = [ordered(ref[i * rows : (i + 1) * rows, :], sizes) for ref, sizes in parts]
        sums.append(sum(x * f for x, f in zip(held, factors)))
        totals.append(sum(x * f for x, f in zip(stat(heads + i), factors)))
    return sums, totals


def project_kernel(swaps, tile, *refs):
    parts, refs = list(zip(refs[: len(swaps)], swaps)), refs[len(swaps) :]
    piece_refs, (send_out, keep_out) = refs[:-2], refs[-2:]
    sums, totals = merged(parts, sum(ref.shape[0] for ref in piece_refs[::2]) // HD)
    attended = jnp.concatenate([a / t for a, t in zip(sums, totals)], axis=1)
    rows = attended.shape[0]
    half = rows // 2
    a1, a2 = pieces_of(attended, 2)
    a12 = jnp.concatenate([a1, a2], axis=0)
    for c in range(keep_out.shape[1] // tile):
        cols = slice(c * tile, (c + 1) * tile)
        out, first = 0.0, 0
        for high_ref, low_ref in zip(piece_refs[::2], piece_refs[1::2]):
            used = slice(first, first + high_ref.shape[0])
            first = used.stop
            top = times(a12[:, used], high_ref[:, cols])
            out = out + (top[:rows] + (top[rows:] + times(a1[:, used], low_ref[:, cols])))
        keep_out[:, cols] = out[:half]
        send_out[:, cols] = out[half:]


def project(swaps, parts, pieces):
    width, heads = pieces[0].shape[1], sum(x.shape[0] for x in pieces[::2]) // HD
    rows = (parts[0].shape[0] - 8) // heads
    out = jax.ShapeDtypeStruct((rows // 2, width), jnp.float32)
    return pl.pallas_call(
        functools.partial(project_kernel, swaps, min(width, 512)),
        out_shape=[out, out],
        in_specs=[IN_VMEM] * (len(parts) + len(pieces)),
        out_specs=[IN_VMEM] * 2,
        compiler_params=limit(16),
        name="project",
    )(*parts, *pieces)


def by_planes(bits, queries, keys, values, weight, lengths):
    blocks = lax.axis_size("blk")
    sub = 1 << bits
    local_rows = queries.shape[0]
    part = KVH * local_rows

    def swap(x, mask):
        return lax.ppermute(x, "blk", [(i, i ^ mask) for i in range(blocks)])

    q_send, limits = pack_q(bits, lengths, queries)
    kv_send = pack_kv(bits, keys, values)
    kv_held = [kv_send[0]] + [swap(kv_send[k], k * sub) for k in range(1, KVH)]
    wide = GROUP * HD
    far = swap(q_send[0], 2 * sub)
    mine = jnp.concatenate([q_send[1], far[:, :wide]], axis=0)
    other = jnp.concatenate([q_send[2], far[:, wide:]], axis=0)
    from_z, from_y = swap(other, sub), swap(mine, 2)
    from_yz = swap(other, 2 + sub)
    q_parts = [jnp.concatenate([mine, from_z], axis=0), jnp.concatenate([from_y, from_yz], axis=0)]
    q_parts = q_parts + [swap(x, 1) for x in q_parts]
    features = weight.shape[0]
    pieces = []
    for i in range(2):
        pieces += split_weight(weight, i * features // 2, features // 2)

    core, side = part << 1, part
    far = attend(bits, (3, 2), limits, q_parts, kv_held)
    near = attend(bits, (1, 0), limits, q_parts, kv_held)
    partials = [near[1], swap(near[0], 1), swap(far[1], 2), swap(far[0], 3)]
    send, keep = project(((), (core,), (side,), (core, side)), partials, pieces)

    recv = swap(send, 1)
    quarter = keep.shape[0] // 4
    rows = [slice(i * quarter, (i + 1) * quarter) for i in range(4)]
    total = keep[rows[0]] + recv[rows[0]]
    for i, mask in ((1, sub), (2, 2), (3, 2 + sub)):
        total = total + swap(keep[rows[i]] + recv[rows[i]], mask)
    out = total[:local_rows] + swap(total[local_rows:], 2 * sub)
    return out


def head_partials(query_rows, keys_held, values_held, key_pos, lengths):
    row_count = query_rows.shape[0]
    grouped = query_rows.reshape(row_count, GROUP, HD)
    scores = jnp.einsum(
        "tje,pe->tjp", grouped, keys_held, precision=HIGHEST, preferred_element_type=jnp.float32
    ) * (1.0 / math.sqrt(HD))
    request_ids = jnp.arange(row_count, dtype=jnp.int32) // REQ_TOK
    request_table = jnp.arange(lengths.shape[0], dtype=jnp.int32)
    limits = jnp.sum(
        jnp.where(request_ids[:, None] == request_table[None, :], lengths[None, :], 0), axis=1
    )
    visible = (key_pos[None, :] < limits[:, None])[:, None, :]
    masked = jnp.where(visible, scores, NEG_FILL)
    peak_vals = jnp.max(masked, axis=2)
    weights = jnp.where(visible, jnp.exp(masked - peak_vals[..., None]), 0.0)
    totals = jnp.sum(weights, axis=2)
    mixed_values = jnp.einsum(
        "tjp,pe->tje", weights, values_held, precision=HIGHEST, preferred_element_type=jnp.float32
    )
    return mixed_values.reshape(row_count, GROUP * HD), peak_vals, totals


def by_all_to_all(queries, keys, values, weight, lengths):
    blocks = lax.axis_size("blk")
    position = lax.axis_index("blk")
    local_rows = queries.shape[0]
    total_rows = local_rows * blocks
    key_count = keys.shape[0]
    sub_count = blocks // KVH
    sub_len = key_count // sub_count

    def exchange(x, split, concat):
        return lax.all_to_all(x, "blk", split_axis=split, concat_axis=concat, tiled=True)

    def spread(x):
        split = x.reshape(sub_count, sub_len, KVH, HD).transpose(0, 2, 1, 3)
        return exchange(split.reshape(blocks, sub_len, HD), 0, 0).reshape(blocks * sub_len, HD)

    held_pos = (
        jnp.arange(blocks, dtype=jnp.int32)[:, None] * key_count
        + position // KVH * sub_len
        + jnp.arange(sub_len, dtype=jnp.int32)[None, :]
    ).reshape(blocks * sub_len)
    query_heads = queries.reshape(local_rows, KVH, GROUP * HD).transpose(1, 0, 2)
    query_send = jnp.broadcast_to(query_heads[None], (sub_count, KVH, local_rows, GROUP * HD))
    query_held = exchange(query_send.reshape(blocks, local_rows, GROUP * HD), 0, 0)
    sums, peaks, totals = head_partials(
        query_held.reshape(total_rows, GROUP * HD), spread(keys), spread(values), held_pos, lengths
    )
    sums = exchange(sums, 0, 0).reshape(sub_count, KVH, local_rows, GROUP, HD)
    peaks = exchange(peaks, 0, 0).reshape(sub_count, KVH, local_rows, GROUP)
    totals = exchange(totals, 0, 0).reshape(sub_count, KVH, local_rows, GROUP)
    factor = jnp.exp(peaks - jnp.max(peaks, axis=0)[None])
    numerator = jnp.sum(sums * factor[..., None], axis=0)
    denominator = jnp.sum(totals * factor, axis=0)
    attended = (numerator / denominator[..., None]).transpose(1, 0, 2, 3).reshape(local_rows, H * HD)
    feature_rows = exchange(attended, 1, 0)
    parts = jnp.dot(feature_rows, weight, precision=HIGHEST, preferred_element_type=jnp.float32)
    return jnp.sum(exchange(parts, 0, 0).reshape(blocks, local_rows, weight.shape[1]), axis=0)


def per_device(queries, prefix_keys, prefix_values, out_weight, lengths):
    blocks = lax.axis_size("blk")
    sub = blocks // KVH
    bits = sub.bit_length() - 1
    fits = (
        blocks == KVH << bits
        and bits == 2
        and PLANE_BITS == 2
        and (KVH * queries.shape[0]) % 8 == 0
        and queries.shape[0] * blocks // 8 * 2 * (GROUP >> bits) <= LANES
        and prefix_keys.shape[0] % LANES == 0
    )
    if fits:
        return by_planes(bits, queries, prefix_keys, prefix_values, out_weight, lengths)
    return by_all_to_all(queries, prefix_keys, prefix_values, out_weight, lengths)


def solution(mesh):
    in_specs = (
        P(("groups", "blk"), None),
        P(("groups", "blk"), None),
        P(("groups", "blk"), None),
        P("blk", None),
        P("groups"),
    )
    out_specs = P(("groups", "blk"), None)
    return jax.shard_map(
        per_device, mesh=mesh, in_specs=in_specs, out_specs=out_specs, check_vma=False
    )
```

profile of v0, /device:TPU:0, one launch (start us, length us, event | category | flops | bytes accessed | tf_op | source)
XLA Modules:
  0.0 49.3 jit_solution(15911527830456802346)
XLA Ops:
  0.0 0.8 %pack_q.1 = (f32[2,4096]{1,0:T(2,128)S(1)}, f32[2,2048]{1,0:T(2,128)S(1)}, f32[2,2048]{1,0:T(2,128)S(1)}, s32[32,128]{1,0:T(8,128)S(1)}) custom-call(s32[2]{0:T(128)} %len_hbm.1, f32[2,8192]{1,0:T(2,128)} %q_hbm.1), custom_call_target="tpu_custom_call" | custom-call | tf_op jit(solution)/shard_map/pack_q/pallas_call | solution.py:113
  0.8 4.1 %collective-permute-start = (f32[2,4096]{1,0:T(2,128)S(1)}, f32[2,4096]{1,0:T(2,128)S(1)}, u32[]{:S(2)}, u32[]{:S(2)}) collective-permute-start(f32[2,4096]{1,0:T(2,128)S(1)} %get-tuple-element.25), channel_id=1, source_target_pairs={{0,8},{1,9},{2,10},{3,11},{4,12},{5,13},{6,14},{7,15},{8,0},{9,1},... | collective-permute-start | bytes 98312 | tf_op jit(solution)/shard_map/ppermute | solution.py:316
  5.0 1.1 %pack_kv.1 = (f32[256,128]{1,0:T(8,128)S(1)}, f32[256,128]{1,0:T(8,128)S(1)}, f32[256,128]{1,0:T(8,128)S(1)}, f32[256,128]{1,0:T(8,128)S(1)}) custom-call(f32[128,512]{1,0:T(8,128)} %k_hbm.1, f32[128,512]{1,0:T(8,128)} %v_hbm.1), custom_call_target="tpu_custom_call" | custom-call | bytes 1048576 | tf_op jit(solution)/shard_map/pack_kv/pallas_call | solution.py:140
  6.1 1.6 %collective-permute-start.6 = (f32[256,128]{1,0:T(8,128)S(1)}, f32[256,128]{1,0:T(8,128)S(1)}, u32[]{:S(2)}, u32[]{:S(2)}) collective-permute-start(f32[256,128]{1,0:T(8,128)S(1)} %get-tuple-element.28), channel_id=1, source_target_pairs={{0,4},{1,5},{2,6},{3,7},{4,0},{5,1},{6,2},{7,3},{8,12},{9,13},{10,... | collective-permute-start | bytes 393224 | tf_op jit(solution)/shard_map/ppermute | solution.py:316
  7.7 0.3 collective-permute-start.7
  8.1 2.5 %collective-permute-start.8 = (f32[256,128]{1,0:T(8,128)S(1)}, f32[256,128]{1,0:T(8,128)S(1)}, u32[]{:S(2)}, u32[]{:S(2)}) collective-permute-start(f32[256,128]{1,0:T(8,128)S(1)} %get-tuple-element.30), channel_id=1, source_target_pairs={{0,12},{1,13},{2,14},{3,15},{4,8},{5,9},{6,10},{7,11},{8,4},{9,5},... | collective-permute-start | bytes 393224 | tf_op jit(solution)/shard_map/ppermute | solution.py:316
  10.6 1.7 %collective-permute-start.3 = (f32[4,2048]{1,0:T(4,128)S(1)}, f32[4,2048]{1,0:T(4,128)S(1)}, u32[]{:S(2)}, u32[]{:S(2)}) collective-permute-start(f32[4,2048]{1,0:T(4,128)S(1)} %pad_maximum_fusion.2), channel_id=1, source_target_pairs={{0,6},{1,7},{2,4},{3,5},{4,2},{5,3},{6,0},{7,1},{8,14},{9,15},{10,... | collective-permute-start | bytes 98312 | tf_op jit(solution)/shard_map/ppermute | solution.py:316
  12.3 1.3 %collective-permute-start.1 = (f32[4,2048]{1,0:T(4,128)S(1)}, f32[4,2048]{1,0:T(4,128)S(1)}, u32[]{:S(2)}, u32[]{:S(2)}) collective-permute-start(f32[4,2048]{1,0:T(4,128)S(1)} %pad_maximum_fusion.2), channel_id=1, source_target_pairs={{0,4},{1,5},{2,6},{3,7},{4,0},{5,1},{6,2},{7,3},{8,12},{9,13},{10,... | collective-permute-start | bytes 98312 | tf_op jit(solution)/shard_map/ppermute | solution.py:316
  13.7 5.9 %collective-permute-done.1 = f32[4,2048]{1,0:T(4,128)S(1)} collective-permute-done((f32[4,2048]{1,0:T(4,128)S(1)}, f32[4,2048]{1,0:T(4,128)S(1)}, u32[]{:S(2)}, u32[]{:S(2)}) %collective-permute-start.1) | collective-permute-done | bytes 32800 | tf_op jit(solution)/shard_map/ppermute | solution.py:316
  19.6 0.7 %collective-permute-start.2 = (f32[4,2048]{1,0:T(4,128)S(1)}, f32[4,2048]{1,0:T(4,128)S(1)}, u32[]{:S(2)}, u32[]{:S(2)}) collective-permute-start(f32[4,2048]{1,0:T(4,128)S(1)} %pad_maximum_fusion.3), channel_id=1, source_target_pairs={{0,2},{1,3},{2,0},{3,1},{4,6},{5,7},{6,4},{7,5},{8,10},{9,11},{10,... | collective-permute-start | bytes 98312 | tf_op jit(solution)/shard_map/ppermute | solution.py:316
  20.3 3.2 %collective-permute-done.2 = f32[4,2048]{1,0:T(4,128)S(1)} collective-permute-done((f32[4,2048]{1,0:T(4,128)S(1)}, f32[4,2048]{1,0:T(4,128)S(1)}, u32[]{:S(2)}, u32[]{:S(2)}) %collective-permute-start.2) | collective-permute-done | bytes 32800 | tf_op jit(solution)/shard_map/ppermute | solution.py:316
  23.5 0.6 %collective-permute-start.5 = (f32[8,2048]{1,0:T(8,128)S(1)}, f32[8,2048]{1,0:T(8,128)S(1)}, u32[]{:S(2)}, u32[]{:S(2)}) collective-permute-start(f32[8,2048]{1,0:T(8,128)S(1)} %pad_maximum_fusion.1.refs_1_), channel_id=1, source_target_pairs={{0,1},{1,0},{2,3},{3,2},{4,5},{5,4},{6,7},{7,6},{8,9},{9,8},{10,11... | collective-permute-start | bytes 196616 | tf_op jit(solution)/shard_map/ppermute | solution.py:316
  24.1 0.7 %collective-permute-done.4.refs_2_ = f32[8,2048]{1,0:T(8,128)S(1)} collective-permute-done((f32[8,2048]{1,0:T(8,128)S(1)}, f32[8,2048]{1,0:T(8,128)S(1)}, u32[]{:S(2)}, u32[]{:S(2)}) %collective-permute-start.4) | collective-permute-done | bytes 65568 | tf_op jit(solution)/shard_map/ppermute | solution.py:316
  24.8 0.2 collective-permute-done.5.refs_3_
  25.0 0.7 %attend.3 = (f32[136,128]{1,0:T(8,128)S(1)}, f32[136,128]{1,0:T(8,128)S(1)}) custom-call(s32[32,128]{1,0:T(8,128)S(1)} %get-tuple-element.23.limit_ref, f32[8,2048]{1,0:T(8,128)S(1)} %pad_maximum_fusion.refs_0_, f32[8,2048]{1,0:T(8,128)S(1)} %pad_maximum_fusion.1.refs_1_, f32[8,2048]{1,0:T(8,128)S(1)} %collective-permute-done.4.refs_2_, ...), custom_call_target="tpu_custom_call" | custom-call | flops 201326592 | bytes 65536 | tf_op jit(solution)/shard_map/attend/pallas_call | solution.py:239
  25.8 0.8 %collective-permute-start.10 = (f32[136,128]{1,0:T(8,128)S(1)}, f32[136,128]{1,0:T(8,128)S(1)}, u32[]{:S(2)}, u32[]{:S(2)}) collective-permute-start(f32[136,128]{1,0:T(8,128)S(1)} %get-tuple-element.33), channel_id=1, source_target_pairs={{0,2},{1,3},{2,0},{3,1},{4,6},{5,7},{6,4},{7,5},{8,10},{9,11},{10,... | collective-permute-start | bytes 208904 | tf_op jit(solution)/shard_map/ppermute | solution.py:316
  26.5 1.0 %collective-permute-start.11 = (f32[136,128]{1,0:T(8,128)S(1)}, f32[136,128]{1,0:T(8,128)S(1)}, u32[]{:S(2)}, u32[]{:S(2)}) collective-permute-start(f32[136,128]{1,0:T(8,128)S(1)} %get-tuple-element.34), channel_id=1, source_target_pairs={{0,3},{1,2},{2,1},{3,0},{4,7},{5,6},{6,5},{7,4},{8,11},{9,10},{10,... | collective-permute-start | bytes 208904 | tf_op jit(solution)/shard_map/ppermute | solution.py:316
  27.5 0.7 %attend.2 = (f32[136,128]{1,0:T(8,128)S(1)}, f32[136,128]{1,0:T(8,128)S(1)}) custom-call(s32[32,128]{1,0:T(8,128)S(1)} %get-tuple-element.23.limit_ref, f32[8,2048]{1,0:T(8,128)S(1)} %pad_maximum_fusion.refs_0_, f32[8,2048]{1,0:T(8,128)S(1)} %pad_maximum_fusion.1.refs_1_, f32[8,2048]{1,0:T(8,128)S(1)} %collective-permute-done.4.refs_2_, ...), custom_call_target="tpu_custom_call" | custom-call | flops 201326592 | bytes 65536 | tf_op jit(solution)/shard_map/attend/pallas_call | solution.py:239
  28.3 0.5 %collective-permute-start.9 = (f32[136,128]{1,0:T(8,128)S(1)}, f32[136,128]{1,0:T(8,128)S(1)}, u32[]{:S(2)}, u32[]{:S(2)}) collective-permute-start(f32[136,128]{1,0:T(8,128)S(1)} %get-tuple-element.32), channel_id=1, source_target_pairs={{0,1},{1,0},{2,3},{3,2},{4,5},{5,4},{6,7},{7,6},{8,9},{9,8},{10,11... | collective-permute-start | bytes 208904 | tf_op jit(solution)/shard_map/ppermute | solution.py:316
  28.8 2.4 %split.3 = (bf16[256,4096]{1,0:T(8,128)(2,1)S(1)}, bf16[256,4096]{1,0:T(8,128)(2,1)S(1)}) custom-call(f32[512,4096]{1,0:T(8,128)} %w_hbm.3), custom_call_target="tpu_custom_call" | custom-call | flops 8388608 | bytes 8388608 | tf_op jit(solution)/shard_map/split/pallas_call | solution.py:170
  31.1 2.4 %split.2 = (bf16[256,4096]{1,0:T(8,128)(2,1)S(1)}, bf16[256,4096]{1,0:T(8,128)(2,1)S(1)}) custom-call(f32[512,4096]{1,0:T(8,128)} %w_hbm.3), custom_call_target="tpu_custom_call" | custom-call | flops 8388608 | bytes 8388608 | tf_op jit(solution)/shard_map/split/pallas_call | solution.py:170
  33.5 1.6 %project.1 = (f32[16,4096]{1,0:T(8,128)S(1)}, f32[16,4096]{1,0:T(8,128)S(1)}) custom-call(f32[136,128]{1,0:T(8,128)S(1)} %get-tuple-element.31.refs_0_, f32[136,128]{1,0:T(8,128)S(1)} %collective-permute-done.9.refs_1_, f32[136,128]{1,0:T(8,128)S(1)} %collective-permute-done.10.refs_2_, f32[136,128]{1,0:T(8,128)S(1)} %collective-permute-done.11.refs_3_, ...), custom_call_target="tpu_custom_call" | custom-call | tf_op jit(solution)/shard_map/project/pallas_call | solution.py:299
  35.2 0.1 collective-permute-start.12
  35.3 1.5 %collective-permute-done.12 = f32[16,4096]{1,0:T(8,128)S(1)} collective-permute-done((f32[16,4096]{1,0:T(8,128)S(1)}, f32[16,4096]{1,0:T(8,128)S(1)}, u32[]{:S(2)}, u32[]{:S(2)}) %collective-permute-start.12) | collective-permute-done | bytes 262176 | tf_op jit(solution)/shard_map/ppermute | solution.py:316
  36.8 0.2 collective-permute-start.13
  37.0 2.0 %collective-permute-start.15 = (f32[4,4096]{1,0:T(4,128)S(1)}, f32[4,4096]{1,0:T(4,128)S(1)}, u32[]{:S(2)}, u32[]{:S(2)}) collective-permute-start(f32[4,4096]{1,0:T(4,128)S(1)} %get-tuple-element.42), channel_id=1, source_target_pairs={{0,6},{1,7},{2,4},{3,5},{4,2},{5,3},{6,0},{7,1},{8,14},{9,15},{10,... | collective-permute-start | bytes 196616 | tf_op jit(solution)/shard_map/ppermute | solution.py:316
  39.0 1.3 %collective-permute-start.14 = (f32[4,4096]{1,0:T(4,128)S(1)}, f32[4,4096]{1,0:T(4,128)S(1)}, u32[]{:S(2)}, u32[]{:S(2)}) collective-permute-start(f32[4,4096]{1,0:T(4,128)S(1)} %get-tuple-element.43), channel_id=1, source_target_pairs={{0,2},{1,3},{2,0},{3,1},{4,6},{5,7},{6,4},{7,5},{8,10},{9,11},{10,... | collective-permute-start | bytes 196616 | tf_op jit(solution)/shard_map/ppermute | solution.py:316
  40.4 1.5 %collective-permute-done.13 = f32[4,4096]{1,0:T(4,128)S(1)} collective-permute-done((f32[4,4096]{1,0:T(4,128)S(1)}, f32[4,4096]{1,0:T(4,128)S(1)}, u32[]{:S(2)}, u32[]{:S(2)}) %collective-permute-start.13) | collective-permute-done | bytes 65568 | tf_op jit(solution)/shard_map/ppermute | solution.py:316
  41.8 0.9 %collective-permute-done.15 = f32[4,4096]{1,0:T(4,128)S(1)} collective-permute-done((f32[4,4096]{1,0:T(4,128)S(1)}, f32[4,4096]{1,0:T(4,128)S(1)}, u32[]{:S(2)}, u32[]{:S(2)}) %collective-permute-start.15) | collective-permute-done | bytes 65568 | tf_op jit(solution)/shard_map/ppermute | solution.py:316
  42.8 0.9 %collective-permute-done.14 = f32[4,4096]{1,0:T(4,128)S(1)} collective-permute-done((f32[4,4096]{1,0:T(4,128)S(1)}, f32[4,4096]{1,0:T(4,128)S(1)}, u32[]{:S(2)}, u32[]{:S(2)}) %collective-permute-start.14) | collective-permute-done | bytes 65568 | tf_op jit(solution)/shard_map/ppermute | solution.py:316
  43.8 4.8 %collective-permute-done.16 = f32[2,4096]{1,0:T(2,128)S(1)} collective-permute-done((f32[2,4096]{1,0:T(2,128)S(1)}, f32[2,4096]{1,0:T(2,128)S(1)}, u32[]{:S(2)}, u32[]{:S(2)}) %collective-permute-start.16) | collective-permute-done | bytes 32800 | tf_op jit(solution)/shard_map/ppermute | solution.py:316
  48.6 0.6 %slice_add_fusion.4 = f32[2,4096]{1,0:T(2,128)} fusion(f32[2,4096]{1,0:T(2,128)S(1)} %collective-permute-done.16, f32[4,4096]{1,0:T(4,128)S(1)} %fusion.2), kind=kLoop, calls=%fused_computation.9 | loop fusion | flops 8192 | bytes 98304 | tf_op jit(solution)/shard_map/add | solution.py:346
  (18 shorter events, 0.3 us)
Async XLA Ops:
  0.8 9.7 %collective-permute-start = (f32[2,4096]{1,0:T(2,128)S(1)}, f32[2,4096]{1,0:T(2,128)S(1)}, u32[]{:S(2)}, u32[]{:S(2)}) collective-permute-start(f32[2,4096]{1,0:T(2,128)S(1)} %get-tuple-element.25), channel_id=1, source_target_pairs={{0,8},{1,9},{2,10},{3,11},{4,12},{5,13},{6,14},{7,15},{8,0},{9,1},... | collective-permute-start | bytes 98312 | tf_op jit(solution)/shard_map/ppermute | solution.py:316
  6.1 18.9 %collective-permute-start.6 = (f32[256,128]{1,0:T(8,128)S(1)}, f32[256,128]{1,0:T(8,128)S(1)}, u32[]{:S(2)}, u32[]{:S(2)}) collective-permute-start(f32[256,128]{1,0:T(8,128)S(1)} %get-tuple-element.28), channel_id=1, source_target_pairs={{0,4},{1,5},{2,6},{3,7},{4,0},{5,1},{6,2},{7,3},{8,12},{9,13},{10,... | collective-permute-start | bytes 393224 | tf_op jit(solution)/shard_map/ppermute | solution.py:316
  7.7 17.3 %collective-permute-start.7 = (f32[256,128]{1,0:T(8,128)S(1)}, f32[256,128]{1,0:T(8,128)S(1)}, u32[]{:S(2)}, u32[]{:S(2)}) collective-permute-start(f32[256,128]{1,0:T(8,128)S(1)} %get-tuple-element.29), channel_id=1, source_target_pairs={{0,8},{1,9},{2,10},{3,11},{4,12},{5,13},{6,14},{7,15},{8,0},{9,1},... | collective-permute-start | bytes 393224 | tf_op jit(solution)/shard_map/ppermute | solution.py:316
  8.1 16.9 %collective-permute-start.8 = (f32[256,128]{1,0:T(8,128)S(1)}, f32[256,128]{1,0:T(8,128)S(1)}, u32[]{:S(2)}, u32[]{:S(2)}) collective-permute-start(f32[256,128]{1,0:T(8,128)S(1)} %get-tuple-element.30), channel_id=1, source_target_pairs={{0,12},{1,13},{2,14},{3,15},{4,8},{5,9},{6,10},{7,11},{8,4},{9,5},... | collective-permute-start | bytes 393224 | tf_op jit(solution)/shard_map/ppermute | solution.py:316
  10.6 12.9 %collective-permute-start.3 = (f32[4,2048]{1,0:T(4,128)S(1)}, f32[4,2048]{1,0:T(4,128)S(1)}, u32[]{:S(2)}, u32[]{:S(2)}) collective-permute-start(f32[4,2048]{1,0:T(4,128)S(1)} %pad_maximum_fusion.2), channel_id=1, source_target_pairs={{0,6},{1,7},{2,4},{3,5},{4,2},{5,3},{6,0},{7,1},{8,14},{9,15},{10,... | collective-permute-start | bytes 98312 | tf_op jit(solution)/shard_map/ppermute | solution.py:316
  12.3 7.3 %collective-permute-start.1 = (f32[4,2048]{1,0:T(4,128)S(1)}, f32[4,2048]{1,0:T(4,128)S(1)}, u32[]{:S(2)}, u32[]{:S(2)}) collective-permute-start(f32[4,2048]{1,0:T(4,128)S(1)} %pad_maximum_fusion.2), channel_id=1, source_target_pairs={{0,4},{1,5},{2,6},{3,7},{4,0},{5,1},{6,2},{7,3},{8,12},{9,13},{10,... | collective-permute-start | bytes 98312 | tf_op jit(solution)/shard_map/ppermute | solution.py:316
  19.6 3.9 %collective-permute-start.2 = (f32[4,2048]{1,0:T(4,128)S(1)}, f32[4,2048]{1,0:T(4,128)S(1)}, u32[]{:S(2)}, u32[]{:S(2)}) collective-permute-start(f32[4,2048]{1,0:T(4,128)S(1)} %pad_maximum_fusion.3), channel_id=1, source_target_pairs={{0,2},{1,3},{2,0},{3,1},{4,6},{5,7},{6,4},{7,5},{8,10},{9,11},{10,... | collective-permute-start | bytes 98312 | tf_op jit(solution)/shard_map/ppermute | solution.py:316
  23.5 1.3 %collective-permute-start.4 = (f32[8,2048]{1,0:T(8,128)S(1)}, f32[8,2048]{1,0:T(8,128)S(1)}, u32[]{:S(2)}, u32[]{:S(2)}) collective-permute-start(f32[8,2048]{1,0:T(8,128)S(1)} %pad_maximum_fusion.refs_0_), channel_id=1, source_target_pairs={{0,1},{1,0},{2,3},{3,2},{4,5},{5,4},{6,7},{7,6},{8,9},{9,8},{10,11... | collective-permute-start | bytes 196616 | tf_op jit(solution)/shard_map/ppermute | solution.py:316
  23.5 1.5 %collective-permute-start.5 = (f32[8,2048]{1,0:T(8,128)S(1)}, f32[8,2048]{1,0:T(8,128)S(1)}, u32[]{:S(2)}, u32[]{:S(2)}) collective-permute-start(f32[8,2048]{1,0:T(8,128)S(1)} %pad_maximum_fusion.1.refs_1_), channel_id=1, source_target_pairs={{0,1},{1,0},{2,3},{3,2},{4,5},{5,4},{6,7},{7,6},{8,9},{9,8},{10,11... | collective-permute-start | bytes 196616 | tf_op jit(solution)/shard_map/ppermute | solution.py:316
  25.8 7.7 %collective-permute-start.10 = (f32[136,128]{1,0:T(8,128)S(1)}, f32[136,128]{1,0:T(8,128)S(1)}, u32[]{:S(2)}, u32[]{:S(2)}) collective-permute-start(f32[136,128]{1,0:T(8,128)S(1)} %get-tuple-element.33), channel_id=1, source_target_pairs={{0,2},{1,3},{2,0},{3,1},{4,6},{5,7},{6,4},{7,5},{8,10},{9,11},{10,... | collective-permute-start | bytes 208904 | tf_op jit(solution)/shard_map/ppermute | solution.py:316
  26.5 7.0 %collective-permute-start.11 = (f32[136,128]{1,0:T(8,128)S(1)}, f32[136,128]{1,0:T(8,128)S(1)}, u32[]{:S(2)}, u32[]{:S(2)}) collective-permute-start(f32[136,128]{1,0:T(8,128)S(1)} %get-tuple-element.34), channel_id=1, source_target_pairs={{0,3},{1,2},{2,1},{3,0},{4,7},{5,6},{6,5},{7,4},{8,11},{9,10},{10,... | collective-permute-start | bytes 208904 | tf_op jit(solution)/shard_map/ppermute | solution.py:316
  28.3 5.3 %collective-permute-start.9 = (f32[136,128]{1,0:T(8,128)S(1)}, f32[136,128]{1,0:T(8,128)S(1)}, u32[]{:S(2)}, u32[]{:S(2)}) collective-permute-start(f32[136,128]{1,0:T(8,128)S(1)} %get-tuple-element.32), channel_id=1, source_target_pairs={{0,1},{1,0},{2,3},{3,2},{4,5},{5,4},{6,7},{7,6},{8,9},{9,8},{10,11... | collective-permute-start | bytes 208904 | tf_op jit(solution)/shard_map/ppermute | solution.py:316
  35.2 1.6 %collective-permute-start.12 = (f32[16,4096]{1,0:T(8,128)S(1)}, f32[16,4096]{1,0:T(8,128)S(1)}, u32[]{:S(2)}, u32[]{:S(2)}) collective-permute-start(f32[16,4096]{1,0:T(8,128)S(1)} %get-tuple-element.40), channel_id=1, source_target_pairs={{0,1},{1,0},{2,3},{3,2},{4,5},{5,4},{6,7},{7,6},{8,9},{9,8},{10,11... | collective-permute-start | bytes 786440 | tf_op jit(solution)/shard_map/ppermute | solution.py:316
  36.8 5.0 %collective-permute-start.13 = (f32[4,4096]{1,0:T(4,128)S(1)}, f32[4,4096]{1,0:T(4,128)S(1)}, u32[]{:S(2)}, u32[]{:S(2)}) collective-permute-start(f32[4,4096]{1,0:T(4,128)S(1)} %get-tuple-element.41), channel_id=1, source_target_pairs={{0,4},{1,5},{2,6},{3,7},{4,0},{5,1},{6,2},{7,3},{8,12},{9,13},{10,... | collective-permute-start | bytes 196616 | tf_op jit(solution)/shard_map/ppermute | solution.py:316
  37.0 5.8 %collective-permute-start.15 = (f32[4,4096]{1,0:T(4,128)S(1)}, f32[4,4096]{1,0:T(4,128)S(1)}, u32[]{:S(2)}, u32[]{:S(2)}) collective-permute-start(f32[4,4096]{1,0:T(4,128)S(1)} %get-tuple-element.42), channel_id=1, source_target_pairs={{0,6},{1,7},{2,4},{3,5},{4,2},{5,3},{6,0},{7,1},{8,14},{9,15},{10,... | collective-permute-start | bytes 196616 | tf_op jit(solution)/shard_map/ppermute | solution.py:316
  39.0 4.7 %collective-permute-start.14 = (f32[4,4096]{1,0:T(4,128)S(1)}, f32[4,4096]{1,0:T(4,128)S(1)}, u32[]{:S(2)}, u32[]{:S(2)}) collective-permute-start(f32[4,4096]{1,0:T(4,128)S(1)} %get-tuple-element.43), channel_id=1, source_target_pairs={{0,2},{1,3},{2,0},{3,1},{4,6},{5,7},{6,4},{7,5},{8,10},{9,11},{10,... | collective-permute-start | bytes 196616 | tf_op jit(solution)/shard_map/ppermute | solution.py:316
  43.8 4.9 %collective-permute-start.16 = (f32[2,4096]{1,0:T(2,128)S(1)}, f32[2,4096]{1,0:T(2,128)S(1)}, u32[]{:S(2)}, u32[]{:S(2)}) collective-permute-start(f32[2,4096]{1,0:T(2,128)S(1)} %slice.55), channel_id=1, source_target_pairs={{0,8},{1,9},{2,10},{3,11},{4,12},{5,13},{6,14},{7,15},{8,0},{9,1},... | collective-permute-start | bytes 98312 | tf_op jit(solution)/shard_map/ppermute | solution.py:316
where the time goes:
time: 49.5 us; the launch traced here: 49.3 us
  waiting for transfers between devices  19.6 us (40%)
  starting transfers between devices  18.9 us (38%)
  Pallas kernels  9.79 us (20%)
  other arithmetic  0.82 us (2%)
    ppermute x17, waiting for transfers between devices, swap(): return lax.ppermute(x, 'blk', [(i, i ^ mask) for i in range(blocks)])  19.6 us
    ppermute x17, starting transfers between devices, swap(): return lax.ppermute(x, 'blk', [(i, i ^ mask) for i in range(blocks)])  18.9 us
    pallas_call x2, Pallas kernels, split_weight(): pl.pallas_call(functools.partial(split_kernel, first, tile), out_shape=[o...  4.71 us
    pallas_call x1, Pallas kernels, project(): pl.pallas_call(functools.partial(project_kernel, swaps, min(width, 512)),...  1.64 us
    pallas_call x2, Pallas kernels, attend(): pl.pallas_call(functools.partial(attend_kernel, bits, key_count, rels), o...  1.49 us
    pallas_call x1, Pallas kernels, pack_kv(): pl.pallas_call(functools.partial(pack_kv_kernel, bits), out_shape=[kv] *...  1.13 us
  transfers between devices with their start and end apart: 17, of which 9 were waited for; matrix products, arithmetic and copies ran while one was open for 0% of the time, Pallas kernels for 13%

commit v1 on v0

--- a/solution.py
+++ b/solution.py
@@ -214,11 +214,11 @@
         for i in range(per_owner):
             lanes = pl.ds(pl.multiple_of(((place ^ rel) * per_owner + i) * HD, HD), HD)
             heads += [q_ref[:, lanes] for q_ref in q_refs]
-    q1, q2, q3 = pieces_of(jnp.concatenate(heads, axis=0), 3)
+    q1, q2, q3 = pieces_of(jnp.concatenate(heads, axis=0) * scale, 3)
     q11, q22 = jnp.concatenate([q1, q1], axis=1), jnp.concatenate([q2, q2], axis=1)
     q13 = jnp.concatenate([q1, q3], axis=1)
     scores = times(q11, k12, both) + (times(q22, k12, both) + times(q13, k31, both))
-    scores = scores.reshape(count, rows, held) * scale
+    scores = scores.reshape(count, rows, held)
     masked = jnp.where(cross, scores, NEG_FILL)
     peak = jnp.max(masked, axis=2, keepdims=True)
     weights = jnp.where(cross, jnp.exp(masked - peak), 0.0)
@@ -319,13 +319,20 @@
     kv_send = pack_kv(bits, keys, values)
     kv_held = [kv_send[0]] + [swap(kv_send[k], k * sub) for k in range(1, KVH)]
     wide = GROUP * HD
-    far = swap(q_send[0], 2 * sub)
-    mine = jnp.concatenate([q_send[1], far[:, :wide]], axis=0)
-    other = jnp.concatenate([q_send[2], far[:, wide:]], axis=0)
-    from_z, from_y = swap(other, sub), swap(mine, 2)
-    from_yz = swap(other, 2 + sub)
-    q_parts = [jnp.concatenate([mine, from_z], axis=0), jnp.concatenate([from_y, from_yz], axis=0)]
-    q_parts = q_parts + [swap(x, 1) for x in q_parts]
+    q_rows = [[q] for q in q_send[1:]]
+    q_out = q_send[0]
+    for b in reversed(range(PLANE_BITS)):
+        q_in = swap(q_out, sub << b)
+        count = len(q_rows[0])
+        got = [q_in[:, i * wide : (i + 1) * wide] for i in range(q_in.shape[1] // wide)]
+        q_rows = [rows + got[t * count : (t + 1) * count] for t, rows in enumerate(q_rows)]
+        high = q_rows[len(q_rows) // 2 :]
+        if b:
+            q_out = jnp.concatenate([piece for rows in high for piece in rows], axis=1)
+            q_rows = q_rows[: len(q_rows) // 2]
+    q_parts = [jnp.concatenate(q_rows[0], axis=0)]
+    for b in reversed(range(bits)):
+        q_parts = q_parts + [swap(x, 1 << b) for x in q_parts]
     features = weight.shape[0]
     pieces = []
     for i in range(2):

time: 49.5 us -> 49 us (0.990)
  waiting for transfers between devices: 19.6 us -> 17.9 us
  starting transfers between devices: 18.9 us -> 20.1 us
    ppermute x17 -> x16, waiting for transfers between devices: 19.6 us -> 17.9 us  [swap(): return lax.ppermute(x, 'blk', [(i, i ^ mask) for i in range(blocks)])]
    ppermute x17 -> x16, starting transfers between devices: 18.9 us -> 20.1 us  [swap(): return lax.ppermute(x, 'blk', [(i, i ^ mask) for i in range(blocks)])]
  transfers between devices with their start and end apart: 17 -> 16, of which waited for: 9 -> 8; matrix products, arithmetic and copies ran while one was open for 0% -> 0% of each run, Pallas kernels for 13% -> 14%
where the time goes in v1:
time: 49 us; the launch traced here: 48.7 us
  starting transfers between devices  20.1 us (41%)
  waiting for transfers between devices  17.9 us (37%)
  Pallas kernels  9.8 us (20%)
  other arithmetic  0.79 us (2%)
    ppermute x16, starting transfers between devices, swap(): return lax.ppermute(x, 'blk', [(i, i ^ mask) for i in range(blocks)])  20.1 us
    ppermute x16, waiting for transfers between devices, swap(): return lax.ppermute(x, 'blk', [(i, i ^ mask) for i in range(blocks)])  17.9 us
    pallas_call x2, Pallas kernels, split_weight(): pl.pallas_call(functools.partial(split_kernel, first, tile), out_shape=[o...  4.71 us
    pallas_call x1, Pallas kernels, project(): pl.pallas_call(functools.partial(project_kernel, swaps, min(width, 512)),...  1.64 us
    pallas_call x2, Pallas kernels, attend(): pl.pallas_call(functools.partial(attend_kernel, bits, key_count, rels), o...  1.5 us
    pallas_call x1, Pallas kernels, pack_kv(): pl.pallas_call(functools.partial(pack_kv_kernel, bits), out_shape=[kv] *...  1.13 us
  transfers between devices with their start and end apart: 16, of which 8 were waited for; matrix products, arithmetic and copies ran while one was open for 0% of the time, Pallas kernels for 14%

profile of v1, /device:TPU:0, one launch (start us, length us, event | category | flops | bytes accessed | tf_op | source)
XLA Modules:
  0.0 48.7 jit_solution(8060616329504322500)
XLA Ops:
  0.0 0.8 %pack_q.1 = (f32[2,4096]{1,0:T(2,128)S(1)}, f32[2,2048]{1,0:T(2,128)S(1)}, f32[2,2048]{1,0:T(2,128)S(1)}, s32[32,128]{1,0:T(8,128)S(1)}) custom-call(s32[2]{0:T(128)} %len_hbm.1, f32[2,8192]{1,0:T(2,128)} %q_hbm.1), custom_call_target="tpu_custom_call" | custom-call | tf_op jit(solution)/shard_map/pack_q/pallas_call | solution.py:113
  0.8 4.1 %collective-permute-start = (f32[2,4096]{1,0:T(2,128)S(1)}, f32[2,4096]{1,0:T(2,128)S(1)}, u32[]{:S(2)}, u32[]{:S(2)}) collective-permute-start(f32[2,4096]{1,0:T(2,128)S(1)} %get-tuple-element.25), channel_id=1, source_target_pairs={{0,8},{1,9},{2,10},{3,11},{4,12},{5,13},{6,14},{7,15},{8,0},{9,1},... | collective-permute-start | bytes 98312 | tf_op jit(solution)/shard_map/ppermute | solution.py:316
  5.0 2.2 %collective-permute-done = f32[2,4096]{1,0:T(2,128)S(1)} collective-permute-done((f32[2,4096]{1,0:T(2,128)S(1)}, f32[2,4096]{1,0:T(2,128)S(1)}, u32[]{:S(2)}, u32[]{:S(2)}) %collective-permute-start) | collective-permute-done | bytes 32800 | tf_op jit(solution)/shard_map/ppermute | solution.py:316
  7.2 1.6 %collective-permute-start.1 = (f32[2,4096]{1,0:T(2,128)S(1)}, f32[2,4096]{1,0:T(2,128)S(1)}, u32[]{:S(2)}, u32[]{:S(2)}) collective-permute-start(f32[2,4096]{1,0:T(2,128)S(1)} %pad_maximum_fusion.1), channel_id=1, source_target_pairs={{0,4},{1,5},{2,6},{3,7},{4,0},{5,1},{6,2},{7,3},{8,12},{9,13},{10,... | collective-permute-start | bytes 98312 | tf_op jit(solution)/shard_map/ppermute | solution.py:316
  8.9 1.1 %pack_kv.1 = (f32[256,128]{1,0:T(8,128)S(1)}, f32[256,128]{1,0:T(8,128)S(1)}, f32[256,128]{1,0:T(8,128)S(1)}, f32[256,128]{1,0:T(8,128)S(1)}) custom-call(f32[128,512]{1,0:T(8,128)} %k_hbm.1, f32[128,512]{1,0:T(8,128)} %v_hbm.1), custom_call_target="tpu_custom_call" | custom-call | bytes 1048576 | tf_op jit(solution)/shard_map/pack_kv/pallas_call | solution.py:140
  10.0 0.5 %collective-permute-start.5 = (f32[256,128]{1,0:T(8,128)S(1)}, f32[256,128]{1,0:T(8,128)S(1)}, u32[]{:S(2)}, u32[]{:S(2)}) collective-permute-start(f32[256,128]{1,0:T(8,128)S(1)} %get-tuple-element.28), channel_id=1, source_target_pairs={{0,4},{1,5},{2,6},{3,7},{4,0},{5,1},{6,2},{7,3},{8,12},{9,13},{10,... | collective-permute-start | bytes 393224 | tf_op jit(solution)/shard_map/ppermute | solution.py:316
  10.5 2.6 %collective-permute-start.6 = (f32[256,128]{1,0:T(8,128)S(1)}, f32[256,128]{1,0:T(8,128)S(1)}, u32[]{:S(2)}, u32[]{:S(2)}) collective-permute-start(f32[256,128]{1,0:T(8,128)S(1)} %get-tuple-element.29), channel_id=1, source_target_pairs={{0,8},{1,9},{2,10},{3,11},{4,12},{5,13},{6,14},{7,15},{8,0},{9,1},... | collective-permute-start | bytes 393224 | tf_op jit(solution)/shard_map/ppermute | solution.py:316
  13.1 1.3 %collective-permute-start.7 = (f32[256,128]{1,0:T(8,128)S(1)}, f32[256,128]{1,0:T(8,128)S(1)}, u32[]{:S(2)}, u32[]{:S(2)}) collective-permute-start(f32[256,128]{1,0:T(8,128)S(1)} %get-tuple-element.30), channel_id=1, source_target_pairs={{0,12},{1,13},{2,14},{3,15},{4,8},{5,9},{6,10},{7,11},{8,4},{9,5},... | collective-permute-start | bytes 393224 | tf_op jit(solution)/shard_map/ppermute | solution.py:316
  14.5 1.6 %collective-permute-start.2 = (f32[8,2048]{1,0:T(8,128)S(1)}, f32[8,2048]{1,0:T(8,128)S(1)}, u32[]{:S(2)}, u32[]{:S(2)}) collective-permute-start(f32[8,2048]{1,0:T(8,128)S(1)} %pad_maximum_fusion.refs_0_), channel_id=1, source_target_pairs={{0,2},{1,3},{2,0},{3,1},{4,6},{5,7},{6,4},{7,5},{8,10},{9,11},{10,... | collective-permute-start | bytes 196616 | tf_op jit(solution)/shard_map/ppermute | solution.py:316
  16.1 2.7 %collective-permute-done.2.refs_1_ = f32[8,2048]{1,0:T(8,128)S(1)} collective-permute-done((f32[8,2048]{1,0:T(8,128)S(1)}, f32[8,2048]{1,0:T(8,128)S(1)}, u32[]{:S(2)}, u32[]{:S(2)}) %collective-permute-start.2) | collective-permute-done | bytes 65568 | tf_op jit(solution)/shard_map/ppermute | solution.py:316
  18.8 0.0 collective-permute-start.4
  18.8 0.0 collective-permute-done.3.refs_2_
  18.8 4.3 %collective-permute-done.6.refs_6_ = f32[256,128]{1,0:T(8,128)S(1)} collective-permute-done((f32[256,128]{1,0:T(8,128)S(1)}, f32[256,128]{1,0:T(8,128)S(1)}, u32[]{:S(2)}, u32[]{:S(2)}) %collective-permute-start.6) | collective-permute-done | bytes 131104 | tf_op jit(solution)/shard_map/ppermute | solution.py:316
  23.2 0.8 %attend.3 = (f32[136,128]{1,0:T(8,128)S(1)}, f32[136,128]{1,0:T(8,128)S(1)}) custom-call(s32[32,128]{1,0:T(8,128)S(1)} %get-tuple-element.23.limit_ref, f32[8,2048]{1,0:T(8,128)S(1)} %pad_maximum_fusion.refs_0_, f32[8,2048]{1,0:T(8,128)S(1)} %collective-permute-done.2.refs_1_, f32[8,2048]{1,0:T(8,128)S(1)} %collective-permute-done.3.refs_2_, ...), custom_call_target="tpu_custom_call" | custom-call | flops 201326592 | bytes 65536 | tf_op jit(solution)/shard_map/attend/pallas_call | solution.py:239
  23.9 1.6 %collective-permute-start.9 = (f32[136,128]{1,0:T(8,128)S(1)}, f32[136,128]{1,0:T(8,128)S(1)}, u32[]{:S(2)}, u32[]{:S(2)}) collective-permute-start(f32[136,128]{1,0:T(8,128)S(1)} %get-tuple-element.33), channel_id=1, source_target_pairs={{0,2},{1,3},{2,0},{3,1},{4,6},{5,7},{6,4},{7,5},{8,10},{9,11},{10,... | collective-permute-start | bytes 208904 | tf_op jit(solution)/shard_map/ppermute | solution.py:316
  25.5 0.7 %attend.2 = (f32[136,128]{1,0:T(8,128)S(1)}, f32[136,128]{1,0:T(8,128)S(1)}) custom-call(s32[32,128]{1,0:T(8,128)S(1)} %get-tuple-element.23.limit_ref, f32[8,2048]{1,0:T(8,128)S(1)} %pad_maximum_fusion.refs_0_, f32[8,2048]{1,0:T(8,128)S(1)} %collective-permute-done.2.refs_1_, f32[8,2048]{1,0:T(8,128)S(1)} %collective-permute-done.3.refs_2_, ...), custom_call_target="tpu_custom_call" | custom-call | flops 201326592 | bytes 65536 | tf_op jit(solution)/shard_map/attend/pallas_call | solution.py:239
  26.2 0.7 %collective-permute-start.8 = (f32[136,128]{1,0:T(8,128)S(1)}, f32[136,128]{1,0:T(8,128)S(1)}, u32[]{:S(2)}, u32[]{:S(2)}) collective-permute-start(f32[136,128]{1,0:T(8,128)S(1)} %get-tuple-element.32), channel_id=1, source_target_pairs={{0,1},{1,0},{2,3},{3,2},{4,5},{5,4},{6,7},{7,6},{8,9},{9,8},{10,11... | collective-permute-start | bytes 208904 | tf_op jit(solution)/shard_map/ppermute | solution.py:316
  26.9 2.4 %split.3 = (bf16[256,4096]{1,0:T(8,128)(2,1)S(1)}, bf16[256,4096]{1,0:T(8,128)(2,1)S(1)}) custom-call(f32[512,4096]{1,0:T(8,128)} %w_hbm.3), custom_call_target="tpu_custom_call" | custom-call | flops 8388608 | bytes 8388608 | tf_op jit(solution)/shard_map/split/pallas_call | solution.py:170
  29.3 2.4 %split.2 = (bf16[256,4096]{1,0:T(8,128)(2,1)S(1)}, bf16[256,4096]{1,0:T(8,128)(2,1)S(1)}) custom-call(f32[512,4096]{1,0:T(8,128)} %w_hbm.3), custom_call_target="tpu_custom_call" | custom-call | flops 8388608 | bytes 8388608 | tf_op jit(solution)/shard_map/split/pallas_call | solution.py:170
  31.7 1.6 %project.1 = (f32[16,4096]{1,0:T(8,128)S(1)}, f32[16,4096]{1,0:T(8,128)S(1)}) custom-call(f32[136,128]{1,0:T(8,128)S(1)} %get-tuple-element.31.refs_0_, f32[136,128]{1,0:T(8,128)S(1)} %collective-permute-done.8.refs_1_, f32[136,128]{1,0:T(8,128)S(1)} %collective-permute-done.9.refs_2_, f32[136,128]{1,0:T(8,128)S(1)} %collective-permute-done.10.refs_3_, ...), custom_call_target="tpu_custom_call" | custom-call | tf_op jit(solution)/shard_map/project/pallas_call | solution.py:299
  33.3 0.0 collective-permute-start.11
  33.4 1.5 %collective-permute-done.11 = f32[16,4096]{1,0:T(8,128)S(1)} collective-permute-done((f32[16,4096]{1,0:T(8,128)S(1)}, f32[16,4096]{1,0:T(8,128)S(1)}, u32[]{:S(2)}, u32[]{:S(2)}) %collective-permute-start.11) | collective-permute-done | bytes 262176 | tf_op jit(solution)/shard_map/ppermute | solution.py:316
  34.9 0.1 slice_add_fusion.2
  34.9 2.0 %collective-permute-start.12 = (f32[4,4096]{1,0:T(4,128)S(1)}, f32[4,4096]{1,0:T(4,128)S(1)}, u32[]{:S(2)}, u32[]{:S(2)}) collective-permute-start(f32[4,4096]{1,0:T(4,128)S(1)} %get-tuple-element.41), channel_id=1, source_target_pairs={{0,4},{1,5},{2,6},{3,7},{4,0},{5,1},{6,2},{7,3},{8,12},{9,13},{10,... | collective-permute-start | bytes 196616 | tf_op jit(solution)/shard_map/ppermute | solution.py:316
  37.0 1.0 %collective-permute-start.14 = (f32[4,4096]{1,0:T(4,128)S(1)}, f32[4,4096]{1,0:T(4,128)S(1)}, u32[]{:S(2)}, u32[]{:S(2)}) collective-permute-start(f32[4,4096]{1,0:T(4,128)S(1)} %get-tuple-element.42), channel_id=1, source_target_pairs={{0,6},{1,7},{2,4},{3,5},{4,2},{5,3},{6,0},{7,1},{8,14},{9,15},{10,... | collective-permute-start | bytes 196616 | tf_op jit(solution)/shard_map/ppermute | solution.py:316
  38.0 0.5 %collective-permute-start.13 = (f32[4,4096]{1,0:T(4,128)S(1)}, f32[4,4096]{1,0:T(4,128)S(1)}, u32[]{:S(2)}, u32[]{:S(2)}) collective-permute-start(f32[4,4096]{1,0:T(4,128)S(1)} %get-tuple-element.43), channel_id=1, source_target_pairs={{0,2},{1,3},{2,0},{3,1},{4,6},{5,7},{6,4},{7,5},{8,10},{9,11},{10,... | collective-permute-start | bytes 196616 | tf_op jit(solution)/shard_map/ppermute | solution.py:316
  38.5 0.9 %collective-permute-done.12 = f32[4,4096]{1,0:T(4,128)S(1)} collective-permute-done((f32[4,4096]{1,0:T(4,128)S(1)}, f32[4,4096]{1,0:T(4,128)S(1)}, u32[]{:S(2)}, u32[]{:S(2)}) %collective-permute-start.12) | collective-permute-done | bytes 65568 | tf_op jit(solution)/shard_map/ppermute | solution.py:316
  39.4 2.8 %collective-permute-done.14 = f32[4,4096]{1,0:T(4,128)S(1)} collective-permute-done((f32[4,4096]{1,0:T(4,128)S(1)}, f32[4,4096]{1,0:T(4,128)S(1)}, u32[]{:S(2)}, u32[]{:S(2)}) %collective-permute-start.14) | collective-permute-done | bytes 65568 | tf_op jit(solution)/shard_map/ppermute | solution.py:316
  42.1 1.0 %collective-permute-done.13 = f32[4,4096]{1,0:T(4,128)S(1)} collective-permute-done((f32[4,4096]{1,0:T(4,128)S(1)}, f32[4,4096]{1,0:T(4,128)S(1)}, u32[]{:S(2)}, u32[]{:S(2)}) %collective-permute-start.13) | collective-permute-done | bytes 65568 | tf_op jit(solution)/shard_map/ppermute | solution.py:316
  43.2 2.4 %collective-permute-start.15 = (f32[2,4096]{1,0:T(2,128)S(1)}, f32[2,4096]{1,0:T(2,128)S(1)}, u32[]{:S(2)}, u32[]{:S(2)}) collective-permute-start(f32[2,4096]{1,0:T(2,128)S(1)} %slice.65), channel_id=1, source_target_pairs={{0,8},{1,9},{2,10},{3,11},{4,12},{5,13},{6,14},{7,15},{8,0},{9,1},... | collective-permute-start | bytes 98312 | tf_op jit(solution)/shard_map/ppermute | solution.py:316
  45.6 2.5 %collective-permute-done.15 = f32[2,4096]{1,0:T(2,128)S(1)} collective-permute-done((f32[2,4096]{1,0:T(2,128)S(1)}, f32[2,4096]{1,0:T(2,128)S(1)}, u32[]{:S(2)}, u32[]{:S(2)}) %collective-permute-start.15) | collective-permute-done | bytes 32800 | tf_op jit(solution)/shard_map/ppermute | solution.py:316
  48.1 0.6 %slice_add_fusion.4 = f32[2,4096]{1,0:T(2,128)} fusion(f32[2,4096]{1,0:T(2,128)S(1)} %collective-permute-done.15, f32[4,4096]{1,0:T(4,128)S(1)} %fusion.2), kind=kLoop, calls=%fused_computation.8 | loop fusion | flops 8192 | bytes 98304 | tf_op jit(solution)/shard_map/add | solution.py:353
  (15 shorter events, 0.1 us)
Async XLA Ops:
  0.8 6.4 %collective-permute-start = (f32[2,4096]{1,0:T(2,128)S(1)}, f32[2,4096]{1,0:T(2,128)S(1)}, u32[]{:S(2)}, u32[]{:S(2)}) collective-permute-start(f32[2,4096]{1,0:T(2,128)S(1)} %get-tuple-element.25), channel_id=1, source_target_pairs={{0,8},{1,9},{2,10},{3,11},{4,12},{5,13},{6,14},{7,15},{8,0},{9,1},... | collective-permute-start | bytes 98312 | tf_op jit(solution)/shard_map/ppermute | solution.py:316
  7.2 7.2 %collective-permute-start.1 = (f32[2,4096]{1,0:T(2,128)S(1)}, f32[2,4096]{1,0:T(2,128)S(1)}, u32[]{:S(2)}, u32[]{:S(2)}) collective-permute-start(f32[2,4096]{1,0:T(2,128)S(1)} %pad_maximum_fusion.1), channel_id=1, source_target_pairs={{0,4},{1,5},{2,6},{3,7},{4,0},{5,1},{6,2},{7,3},{8,12},{9,13},{10,... | collective-permute-start | bytes 98312 | tf_op jit(solution)/shard_map/ppermute | solution.py:316
  10.0 8.8 %collective-permute-start.5 = (f32[256,128]{1,0:T(8,128)S(1)}, f32[256,128]{1,0:T(8,128)S(1)}, u32[]{:S(2)}, u32[]{:S(2)}) collective-permute-start(f32[256,128]{1,0:T(8,128)S(1)} %get-tuple-element.28), channel_id=1, source_target_pairs={{0,4},{1,5},{2,6},{3,7},{4,0},{5,1},{6,2},{7,3},{8,12},{9,13},{10,... | collective-permute-start | bytes 393224 | tf_op jit(solution)/shard_map/ppermute | solution.py:316
  10.5 12.6 %collective-permute-start.6 = (f32[256,128]{1,0:T(8,128)S(1)}, f32[256,128]{1,0:T(8,128)S(1)}, u32[]{:S(2)}, u32[]{:S(2)}) collective-permute-start(f32[256,128]{1,0:T(8,128)S(1)} %get-tuple-element.29), channel_id=1, source_target_pairs={{0,8},{1,9},{2,10},{3,11},{4,12},{5,13},{6,14},{7,15},{8,0},{9,1},... | collective-permute-start | bytes 393224 | tf_op jit(solution)/shard_map/ppermute | solution.py:316
  13.1 10.0 %collective-permute-start.7 = (f32[256,128]{1,0:T(8,128)S(1)}, f32[256,128]{1,0:T(8,128)S(1)}, u32[]{:S(2)}, u32[]{:S(2)}) collective-permute-start(f32[256,128]{1,0:T(8,128)S(1)} %get-tuple-element.30), channel_id=1, source_target_pairs={{0,12},{1,13},{2,14},{3,15},{4,8},{5,9},{6,10},{7,11},{8,4},{9,5},... | collective-permute-start | bytes 393224 | tf_op jit(solution)/shard_map/ppermute | solution.py:316
  14.5 4.3 %collective-permute-start.2 = (f32[8,2048]{1,0:T(8,128)S(1)}, f32[8,2048]{1,0:T(8,128)S(1)}, u32[]{:S(2)}, u32[]{:S(2)}) collective-permute-start(f32[8,2048]{1,0:T(8,128)S(1)} %pad_maximum_fusion.refs_0_), channel_id=1, source_target_pairs={{0,2},{1,3},{2,0},{3,1},{4,6},{5,7},{6,4},{7,5},{8,10},{9,11},{10,... | collective-permute-start | bytes 196616 | tf_op jit(solution)/shard_map/ppermute | solution.py:316
  16.1 2.8 %collective-permute-start.3 = (f32[8,2048]{1,0:T(8,128)S(1)}, f32[8,2048]{1,0:T(8,128)S(1)}, u32[]{:S(2)}, u32[]{:S(2)}) collective-permute-start(f32[8,2048]{1,0:T(8,128)S(1)} %pad_maximum_fusion.refs_0_), channel_id=1, source_target_pairs={{0,1},{1,0},{2,3},{3,2},{4,5},{5,4},{6,7},{7,6},{8,9},{9,8},{10,11... | collective-permute-start | bytes 196616 | tf_op jit(solution)/shard_map/ppermute | solution.py:316
  18.8 4.3 %collective-permute-start.4 = (f32[8,2048]{1,0:T(8,128)S(1)}, f32[8,2048]{1,0:T(8,128)S(1)}, u32[]{:S(2)}, u32[]{:S(2)}) collective-permute-start(f32[8,2048]{1,0:T(8,128)S(1)} %collective-permute-done.2.refs_1_), channel_id=1, source_target_pairs={{0,1},{1,0},{2,3},{3,2},{4,5},{5,4},{6,7},{7,6},{8,9},{9,8},{10,11... | collective-permute-start | bytes 196616 | tf_op jit(solution)/shard_map/ppermute | solution.py:316
  23.9 7.8 %collective-permute-start.9 = (f32[136,128]{1,0:T(8,128)S(1)}, f32[136,128]{1,0:T(8,128)S(1)}, u32[]{:S(2)}, u32[]{:S(2)}) collective-permute-start(f32[136,128]{1,0:T(8,128)S(1)} %get-tuple-element.33), channel_id=1, source_target_pairs={{0,2},{1,3},{2,0},{3,1},{4,6},{5,7},{6,4},{7,5},{8,10},{9,11},{10,... | collective-permute-start | bytes 208904 | tf_op jit(solution)/shard_map/ppermute | solution.py:316
  25.5 6.2 %collective-permute-start.10 = (f32[136,128]{1,0:T(8,128)S(1)}, f32[136,128]{1,0:T(8,128)S(1)}, u32[]{:S(2)}, u32[]{:S(2)}) collective-permute-start(f32[136,128]{1,0:T(8,128)S(1)} %get-tuple-element.34), channel_id=1, source_target_pairs={{0,3},{1,2},{2,1},{3,0},{4,7},{5,6},{6,5},{7,4},{8,11},{9,10},{10,... | collective-permute-start | bytes 208904 | tf_op jit(solution)/shard_map/ppermute | solution.py:316
  26.2 5.4 %collective-permute-start.8 = (f32[136,128]{1,0:T(8,128)S(1)}, f32[136,128]{1,0:T(8,128)S(1)}, u32[]{:S(2)}, u32[]{:S(2)}) collective-permute-start(f32[136,128]{1,0:T(8,128)S(1)} %get-tuple-element.32), channel_id=1, source_target_pairs={{0,1},{1,0},{2,3},{3,2},{4,5},{5,4},{6,7},{7,6},{8,9},{9,8},{10,11... | collective-permute-start | bytes 208904 | tf_op jit(solution)/shard_map/ppermute | solution.py:316
  33.3 1.6 %collective-permute-start.11 = (f32[16,4096]{1,0:T(8,128)S(1)}, f32[16,4096]{1,0:T(8,128)S(1)}, u32[]{:S(2)}, u32[]{:S(2)}) collective-permute-start(f32[16,4096]{1,0:T(8,128)S(1)} %get-tuple-element.40), channel_id=1, source_target_pairs={{0,1},{1,0},{2,3},{3,2},{4,5},{5,4},{6,7},{7,6},{8,9},{9,8},{10,11... | collective-permute-start | bytes 786440 | tf_op jit(solution)/shard_map/ppermute | solution.py:316
  34.9 4.4 %collective-permute-start.12 = (f32[4,4096]{1,0:T(4,128)S(1)}, f32[4,4096]{1,0:T(4,128)S(1)}, u32[]{:S(2)}, u32[]{:S(2)}) collective-permute-start(f32[4,4096]{1,0:T(4,128)S(1)} %get-tuple-element.41), channel_id=1, source_target_pairs={{0,4},{1,5},{2,6},{3,7},{4,0},{5,1},{6,2},{7,3},{8,12},{9,13},{10,... | collective-permute-start | bytes 196616 | tf_op jit(solution)/shard_map/ppermute | solution.py:316
  37.0 5.2 %collective-permute-start.14 = (f32[4,4096]{1,0:T(4,128)S(1)}, f32[4,4096]{1,0:T(4,128)S(1)}, u32[]{:S(2)}, u32[]{:S(2)}) collective-permute-start(f32[4,4096]{1,0:T(4,128)S(1)} %get-tuple-element.42), channel_id=1, source_target_pairs={{0,6},{1,7},{2,4},{3,5},{4,2},{5,3},{6,0},{7,1},{8,14},{9,15},{10,... | collective-permute-start | bytes 196616 | tf_op jit(solution)/shard_map/ppermute | solution.py:316
  38.0 5.1 %collective-permute-start.13 = (f32[4,4096]{1,0:T(4,128)S(1)}, f32[4,4096]{1,0:T(4,128)S(1)}, u32[]{:S(2)}, u32[]{:S(2)}) collective-permute-start(f32[4,4096]{1,0:T(4,128)S(1)} %get-tuple-element.43), channel_id=1, source_target_pairs={{0,2},{1,3},{2,0},{3,1},{4,6},{5,7},{6,4},{7,5},{8,10},{9,11},{10,... | collective-permute-start | bytes 196616 | tf_op jit(solution)/shard_map/ppermute | solution.py:316
  43.2 4.9 %collective-permute-start.15 = (f32[2,4096]{1,0:T(2,128)S(1)}, f32[2,4096]{1,0:T(2,128)S(1)}, u32[]{:S(2)}, u32[]{:S(2)}) collective-permute-start(f32[2,4096]{1,0:T(2,128)S(1)} %slice.65), channel_id=1, source_target_pairs={{0,8},{1,9},{2,10},{3,11},{4,12},{5,13},{6,14},{7,15},{8,0},{9,1},... | collective-permute-start | bytes 98312 | tf_op jit(solution)/shard_map/ppermute | solution.py:316
